TPU v7x, 32 devices: a whole 2x2x4 slice. The times are simulated.
32 devices in a mesh: fsdp: 32 (over z, y, x, core).
Axes of the slice: x: 2, y: 2, z: 4, core: 2. Of those that a mesh axis runs over, the one named last changes fastest.
Arguments:
- tokens: bfloat16 [16384, 1024], P('fsdp'), may hold values from -6 to 6
- out_grad: bfloat16 [16384, 1024], P('fsdp'), may hold values from -6 to 6
- segments: int32 [16384], replicated, may hold values from 0 to 63, never falling along the last dimension, each value on 1 to 512 neighbouring positions
- seq_lengths: int32 [4], replicated, may hold values from 1 to 8192, 16384 in all
- ln1_gain: bfloat16 [1024], P('fsdp'), may hold values from 0.5 to 1.5
- ln1_bias: bfloat16 [1024], P('fsdp'), may hold values from -3 to 3
- w_qkv: bfloat16 [1024, 3072], P('fsdp'), may hold values from -0.1875 to 0.1875
- b_qv: bfloat16 [2048], P('fsdp'), may hold values from -3 to 3
- w_out: bfloat16 [1024, 1024], P('fsdp'), may hold values from -0.75 to 0.75
- b_out: bfloat16 [1024], P('fsdp'), may hold values from -3 to 3
- ln2_gain: bfloat16 [1024], P('fsdp'), may hold values from 0.5 to 1.5
- ln2_bias: bfloat16 [1024], P('fsdp'), may hold values from -3 to 3
- w_fc: bfloat16 [1024, 4096], P('fsdp'), may hold values from -0.1875 to 0.1875
- b_fc: bfloat16 [4096], P('fsdp'), may hold values from -3 to 3
- w_proj: bfloat16 [4096, 1024], P('fsdp'), may hold values from -0.09375 to 0.09375
- b_proj: bfloat16 [1024], P('fsdp'), may hold values from -3 to 3
Outputs:
- block_out: bfloat16 [16384, 1024], P('fsdp')
- tokens_grad: float32 [16384, 1024], P('fsdp')
- ln1_gain_grad: float32 [1024], P('fsdp')
- ln1_bias_grad: float32 [1024], P('fsdp')
- w_qkv_grad: float32 [1024, 3072], P('fsdp')
- b_qv_grad: float32 [2048], P('fsdp')
- w_out_grad: float32 [1024, 1024], P('fsdp')
- b_out_grad: float32 [1024], P('fsdp')
- ln2_gain_grad: float32 [1024], P('fsdp')
- ln2_bias_grad: float32 [1024], P('fsdp')
- w_fc_grad: float32 [1024, 4096], P('fsdp')
- b_fc_grad: float32 [4096], P('fsdp')
- w_proj_grad: float32 [4096, 1024], P('fsdp')
- b_proj_grad: float32 [1024], P('fsdp')
Inputs may be any that keep to these rules, and one draw needn't show every extreme that they name: `segments`: document numbers never fall along the token stream; every document number is used, by 1 to 512 consecutive tokens, and one document has exactly 512. `seq_lengths`: the sequences lie end to end from token 0 and their lengths sum to 16384; the longest has exactly half of 16384.
All inputs are finite; a program needn't handle non-finite values.
Results may differ from a plain program's by a relative error of at most 0.011.
Values may be sent and summed in bfloat16 or wider, within the bound.
No kernel may reach another device: no remote copies, remote signals or barrier semaphores. Data moves between devices by JAX's collectives and lax.ppermute only.
A program may use at most 192 MiB of HBM per device.

v0:
```python
import jax
import jax.numpy as jnp
from jax import lax
from jax.sharding import PartitionSpec as P

HEAD_DIM = 64
SEQ = 512


NORM_EPS = 1e-05
GELU_COEF = 0.7978845608028654
GELU_CUBIC = 0.044715
MASK_FILL = -1e30


def from_behind(value, axis, steps):
    count = lax.axis_size(axis)
    initial, last = (max(0, -steps), min(count, count - steps))
    return lax.ppermute(value, axis, [(source, source + steps) for source in range(initial, last)])


def times_plain(left, right):
    return jnp.dot(left, right, preferred_element_type=jnp.float32)


def times_left_t(left, right):
    return lax.dot_general(
        left, right, (((0,), (0,)), ((), ())), preferred_element_type=jnp.float32
    )


def times_right_t(left, right):
    return lax.dot_general(
        left, right, (((1,), (1,)), ((), ())), preferred_element_type=jnp.float32
    )


def norm_parts(values):
    centre = jnp.mean(values, axis=-1, keepdims=True)
    centered = values - centre
    inverse = lax.rsqrt(jnp.mean(centered * centered, axis=-1, keepdims=True) + NORM_EPS)
    return (centered * inverse, inverse)


def norm_back(grad_out, normed, inverse, gain_row):
    scaled = grad_out * gain_row
    return inverse * (
        scaled
        - jnp.mean(scaled, axis=-1, keepdims=True)
        - normed * jnp.mean(scaled * normed, axis=-1, keepdims=True)
    )


def merge_heads(stacked, model_width):
    return jnp.transpose(stacked, (1, 0, 2)).reshape(stacked.shape[1], model_width)


def on_device(
    tokens,
    out_grad,
    segments,
    seq_lengths,
    ln1_gain,
    ln1_bias,
    w_qkv,
    b_qv,
    w_out,
    b_out,
    ln2_gain,
    ln2_bias,
    w_fc,
    b_fc,
    w_proj,
    b_proj,
):
    tok_rows = tokens.shape[0]
    model_width = tokens.shape[1]
    head_count = model_width // HEAD_DIM
    prior_count = (SEQ - 2) // tok_rows + 1
    window_rows = (prior_count + 1) * tok_rows
    scale_factor = HEAD_DIM ** (-0.5)
    fetched = (
        lax.all_gather(ln1_gain, "fsdp", axis=0, tiled=True),
        lax.all_gather(ln1_bias, "fsdp", axis=0, tiled=True),
        lax.all_gather(w_qkv, "fsdp", axis=0, tiled=True),
        lax.all_gather(b_qv, "fsdp", axis=0, tiled=True),
        lax.all_gather(w_out, "fsdp", axis=0, tiled=True),
        lax.all_gather(b_out, "fsdp", axis=0, tiled=True),
        lax.all_gather(ln2_gain, "fsdp", axis=0, tiled=True),
        lax.all_gather(ln2_bias, "fsdp", axis=0, tiled=True),
        lax.all_gather(w_fc, "fsdp", axis=0, tiled=True),
        lax.all_gather(b_fc, "fsdp", axis=0, tiled=True),
        lax.all_gather(w_proj, "fsdp", axis=0, tiled=True),
        lax.all_gather(b_proj, "fsdp", axis=0, tiled=True),
    )
    (
        gain_one,
        shift_one,
        qkv_full,
        qv_bias,
        out_full,
        out_bias,
        gain_two,
        shift_two,
        fc_full,
        fc_bias,
        proj_full,
        proj_bias,
    ) = fetched
    gain_one = gain_one.astype(jnp.float32)
    shift_one = shift_one.astype(jnp.float32)
    gain_two = gain_two.astype(jnp.float32)
    shift_two = shift_two.astype(jnp.float32)
    device_index = lax.axis_index("fsdp")
    first_row = device_index * tok_rows
    padded_seg = jnp.concatenate([jnp.full((prior_count * tok_rows,), -1, jnp.int32), segments])
    key_seg = lax.dynamic_slice_in_dim(padded_seg, first_row, window_rows, 0)
    query_seg = lax.dynamic_slice_in_dim(segments, first_row, tok_rows, 0)
    query_pos = first_row + jnp.arange(tok_rows, dtype=jnp.int32)
    key_pos = first_row - prior_count * tok_rows + jnp.arange(window_rows, dtype=jnp.int32)
    seq_ends = jnp.cumsum(seq_lengths)
    query_seq = jnp.sum((query_pos[:, None] >= seq_ends[None, :]).astype(jnp.int32), axis=1)
    key_seq = jnp.sum((key_pos[:, None] >= seq_ends[None, :]).astype(jnp.int32), axis=1)
    allowed = (query_seg[:, None] == key_seg[None, :]) & (query_seq[:, None] == key_seq[None, :])
    allowed = allowed & (key_pos[None, :] <= query_pos[:, None]) & (key_pos[None, :] >= 0)
    tokens_f = tokens.astype(jnp.float32)
    normed_one, inverse_one = norm_parts(tokens_f)
    hidden_one = (normed_one * gain_one + shift_one).astype(jnp.bfloat16)
    qv_bias_f = qv_bias.astype(jnp.float32)
    bias_full = jnp.concatenate(
        [qv_bias_f[:model_width], jnp.zeros((model_width,), jnp.float32), qv_bias_f[model_width:]]
    )
    qkv = (times_plain(hidden_one, qkv_full) + bias_full).astype(jnp.bfloat16)
    query = qkv[:, :model_width]
    keys = qkv[:, model_width : 2 * model_width]
    values = qkv[:, 2 * model_width :]
    offset = 1
    moved_keys, moved_values = from_behind((keys, values), "fsdp", offset)
    key_parts = [moved_keys]
    value_parts = [moved_values]
    key_window = jnp.concatenate(key_parts + [keys], axis=0)
    value_window = jnp.concatenate(value_parts + [values], axis=0)

    def head_forward(head_index):
        column = head_index * HEAD_DIM
        q_head = lax.dynamic_slice_in_dim(query, column, HEAD_DIM, 1)
        k_head = lax.dynamic_slice_in_dim(key_window, column, HEAD_DIM, 1)
        v_head = lax.dynamic_slice_in_dim(value_window, column, HEAD_DIM, 1)
        raw_scores = times_right_t(q_head, k_head) * scale_factor
        masked = jnp.where(allowed, raw_scores, MASK_FILL)
        top_score = jnp.max(masked, axis=1, keepdims=True)
        expo = jnp.exp(masked - top_score)
        row_total = jnp.sum(expo, axis=1, keepdims=True)
        probs = (expo / row_total).astype(jnp.bfloat16)
        return (times_plain(probs, v_head), (top_score + jnp.log(row_total))[:, 0])

    head_outputs, log_sums = lax.map(head_forward, jnp.arange(head_count, dtype=jnp.int32))
    attended = merge_heads(head_outputs, model_width).astype(jnp.bfloat16)
    resid = tokens_f + times_plain(attended, out_full) + out_bias.astype(jnp.float32)
    normed_two, inverse_two = norm_parts(resid)
    hidden_two = (normed_two * gain_two + shift_two).astype(jnp.bfloat16)
    pre = times_plain(hidden_two, fc_full) + fc_bias.astype(jnp.float32)
    tanh_part = jnp.tanh(GELU_COEF * (pre + GELU_CUBIC * pre * pre * pre))
    act = (0.5 * pre * (1.0 + tanh_part)).astype(jnp.bfloat16)
    result = (resid + times_plain(act, proj_full) + proj_bias.astype(jnp.float32)).astype(
        jnp.bfloat16
    )
    again = (
        lax.all_gather(ln1_gain, "fsdp", axis=0, tiled=True),
        lax.all_gather(w_qkv, "fsdp", axis=0, tiled=True),
        lax.all_gather(w_out, "fsdp", axis=0, tiled=True),
        lax.all_gather(ln2_gain, "fsdp", axis=0, tiled=True),
        lax.all_gather(w_fc, "fsdp", axis=0, tiled=True),
        lax.all_gather(w_proj, "fsdp", axis=0, tiled=True),
    )
    gain_back_one = again[0].astype(jnp.float32)
    qkv_back, out_back = (again[1], again[2])
    gain_back_two = again[3].astype(jnp.float32)
    fc_back, proj_back = (again[4], again[5])
    grad_top = out_grad.astype(jnp.float32)
    proj_w_grad = times_left_t(act, out_grad)
    proj_b_grad = jnp.sum(grad_top, axis=0)
    grad_act = times_right_t(out_grad, proj_back)
    slope = 0.5 * (1.0 + tanh_part) + 0.5 * pre * (1.0 - tanh_part * tanh_part) * GELU_COEF * (
        1.0 + 3.0 * GELU_CUBIC * pre * pre
    )
    grad_pre = (grad_act * slope).astype(jnp.bfloat16)
    fc_w_grad = times_left_t(hidden_two, grad_pre)
    fc_b_grad = jnp.sum(grad_pre.astype(jnp.float32), axis=0)
    grad_hidden_two = times_right_t(grad_pre, fc_back)
    gain_two_grad = jnp.sum(grad_hidden_two * normed_two, axis=0)
    shift_two_grad = jnp.sum(grad_hidden_two, axis=0)
    grad_resid = grad_top + norm_back(grad_hidden_two, normed_two, inverse_two, gain_back_two)
    grad_branch = grad_resid.astype(jnp.bfloat16)
    out_w_grad = times_left_t(attended, grad_branch)
    out_b_grad = jnp.sum(grad_branch.astype(jnp.float32), axis=0)
    grad_att = times_right_t(grad_branch, out_back).astype(jnp.bfloat16)

    def head_backward(inputs):
        head_index, log_sum = inputs
        column = head_index * HEAD_DIM
        q_head = lax.dynamic_slice_in_dim(query, column, HEAD_DIM, 1)
        k_head = lax.dynamic_slice_in_dim(key_window, column, HEAD_DIM, 1)
        v_head = lax.dynamic_slice_in_dim(value_window, column, HEAD_DIM, 1)
        g_head = lax.dynamic_slice_in_dim(grad_att, column, HEAD_DIM, 1)
        raw_scores = times_right_t(q_head, k_head) * scale_factor
        masked = jnp.where(allowed, raw_scores, MASK_FILL)
        probs_full = jnp.exp(masked - log_sum[:, None])
        grad_probs = times_right_t(g_head, v_head)
        delta_row = jnp.sum(probs_full * grad_probs, axis=1, keepdims=True)
        grad_scores = (probs_full * (grad_probs - delta_row)).astype(jnp.bfloat16)
        grad_query = times_plain(grad_scores, k_head) * scale_factor
        grad_key = times_left_t(grad_scores, q_head) * scale_factor
        grad_value = times_left_t(probs_full.astype(jnp.bfloat16), g_head)
        return (grad_query, grad_key, grad_value)

    query_grads, key_grads, value_grads = lax.map(
        head_backward, (jnp.arange(head_count, dtype=jnp.int32), log_sums)
    )
    query_grad = merge_heads(query_grads, model_width)
    key_grad_all = merge_heads(key_grads, model_width)
    value_grad_all = merge_heads(value_grads, model_width)
    own_start = prior_count * tok_rows
    key_grad = key_grad_all[own_start:]
    value_grad = value_grad_all[own_start:]
    offset = 1
    begin = (prior_count - offset) * tok_rows
    back_keys = from_behind(
        key_grad_all[begin : begin + tok_rows].astype(jnp.bfloat16), "fsdp", -offset
    ).astype(jnp.float32)
    back_values = from_behind(
        value_grad_all[begin : begin + tok_rows].astype(jnp.bfloat16), "fsdp", -offset
    ).astype(jnp.float32)
    key_grad = key_grad + back_keys
    value_grad = value_grad + back_values
    grad_qkv = jnp.concatenate([query_grad, key_grad, value_grad], axis=1).astype(jnp.bfloat16)
    qkv_w_grad = times_left_t(hidden_one, grad_qkv)
    column_sums = jnp.sum(grad_qkv.astype(jnp.float32), axis=0)
    qv_b_grad = jnp.concatenate([column_sums[:model_width], column_sums[2 * model_width :]])
    grad_hidden_one = times_right_t(grad_qkv, qkv_back)
    gain_one_grad = jnp.sum(grad_hidden_one * normed_one, axis=0)
    shift_one_grad = jnp.sum(grad_hidden_one, axis=0)
    tokens_grad = grad_resid + norm_back(grad_hidden_one, normed_one, inverse_one, gain_back_one)
    all_shares = (
        lax.psum_scatter(gain_one_grad, "fsdp", scatter_dimension=0, tiled=True),
        lax.psum_scatter(shift_one_grad, "fsdp", scatter_dimension=0, tiled=True),
        lax.psum_scatter(qkv_w_grad, "fsdp", scatter_dimension=0, tiled=True),
        lax.psum_scatter(qv_b_grad, "fsdp", scatter_dimension=0, tiled=True),
        lax.psum_scatter(out_w_grad, "fsdp", scatter_dimension=0, tiled=True),
        lax.psum_scatter(out_b_grad, "fsdp", scatter_dimension=0, tiled=True),
        lax.psum_scatter(gain_two_grad, "fsdp", scatter_dimension=0, tiled=True),
        lax.psum_scatter(shift_two_grad, "fsdp", scatter_dimension=0, tiled=True),
        lax.psum_scatter(fc_w_grad, "fsdp", scatter_dimension=0, tiled=True),
        lax.psum_scatter(fc_b_grad, "fsdp", scatter_dimension=0, tiled=True),
        lax.psum_scatter(proj_w_grad, "fsdp", scatter_dimension=0, tiled=True),
        lax.psum_scatter(proj_b_grad, "fsdp", scatter_dimension=0, tiled=True),
    )
    return (
        result,
        tokens_grad,
        all_shares[0],
        all_shares[1],
        all_shares[2],
        all_shares[3],
        all_shares[4],
        all_shares[5],
        all_shares[6],
        all_shares[7],
        all_shares[8],
        all_shares[9],
        all_shares[10],
        all_shares[11],
    )


def solution(mesh):
    return jax.shard_map(
        on_device,
        mesh=mesh,
        in_specs=(
            P("fsdp", None),
            P("fsdp", None),
            P(),
            P(),
            P("fsdp"),
            P("fsdp"),
            P("fsdp", None),
            P("fsdp"),
            P("fsdp", None),
            P("fsdp"),
            P("fsdp"),
            P("fsdp"),
            P("fsdp", None),
            P("fsdp"),
            P("fsdp", None),
            P("fsdp"),
        ),
        out_specs=(
            P("fsdp", None),
            P("fsdp", None),
            P("fsdp"),
            P("fsdp"),
            P("fsdp", None),
            P("fsdp"),
            P("fsdp", None),
            P("fsdp"),
            P("fsdp"),
            P("fsdp"),
            P("fsdp", None),
            P("fsdp"),
            P("fsdp", None),
            P("fsdp"),
        ),
        check_vma=False,
    )
```

profile of v0, /device:TPU:13, one launch (start us, length us, event | category | flops | bytes accessed | tf_op | source)
XLA Modules:
  0.0 1094.5 jit_solution(10813405021007344984)
XLA Ops:
  15.3 39.7 %all-reduce.17 = (bf16[2048]{0:T(1024)(128)(2,1)S(1)}, bf16[1024]{0:T(1024)(128)(2,1)S(1)}, bf16[1024]{0:T(1024)(128)(2,1)S(1)}, bf16[1024]{0:T(1024)(128)(2,1)S...) all-reduce(bf16[2048]{0:T(1024)(128)(2,1)S(1)} %dynamic-update-slic, ...), channel_id=1, replica_groups=mesh['fsdp'=32] {'fsdp'}, use_global_device_ids=true, to_apply=%add.3 | all-reduce | flops 8192 | bytes 32768
  57.0 24.7 %all-gather.6.cloned.1.call-done = bf16[1024,3072]{1,0:T(8,128)(2,1)} async-done(((bf16[32,3072]{1,0:T(8,128)(2,1)}), bf16[1024,3072]{1,0:T(8,128)(2,1)}) %all-gather.6.cloned.1.call-update) | async-done | bytes 6291472 | tf_op jit(solution)/shard_map/all_gather | solution.py:85
  81.7 6.7 add_convert_fusion
  94.6 48.7 %all-gather = bf16[32,1,128]{2,1,0:T(2,128)(2,1)S(1)} all-gather(bf16[1,1,128]{2,1,0:T(2,128)(2,1)S(1)} %bitcast.96), channel_id=1, replica_groups=mesh['fsdp'=32] {'fsdp'}, dimensions={0}, use_global_device_ids=true | all-gather | bytes 8448 | tf_op jit(solution)/shard_map/all_gather | solution.py:92
  143.7 2.7 pad_maximum_fusion.1
  146.4 2.7 pad_maximum_fusion.2
  149.3 89.9 %while.28 = (s32[]{:T(128)}, bf16[16,512,64]{1,2,0:T(8,128)(2,1)S(1)}, f32[16,512]{1,0:T(8,128)S(1)}, s32[16]{0:T(128)S(1)}, bf16[512,1024]{1,0:T(8,128)(2,1)}, ...) while((s32[]{:T(128)}, ...), condition=%wide.region_8.9_spmd.clone, body=%wide.region_5.8_spmd.clone.sunk | while | flops 141557248 | bytes 7119091 | solution.py:157
  240.2 3.3 fusion.69
  243.9 10.6 fusion.63
  254.4 46.3 %all-gather.12.cloned.1.call-done = bf16[4096,1024]{1,0:T(8,128)(2,1)} async-done(((bf16[128,1024]{1,0:T(8,128)(2,1)}), bf16[4096,1024]{1,0:T(8,128)(2,1)}) %all-gather.12.cloned.1.call-update) | async-done | bytes 8388624 | tf_op jit(solution)/shard_map/all_gather | solution.py:93
  300.7 13.2 %convert_reduce_fusion = (f32[4096]{0:T(1024)S(1)}, bf16[512,4096]{1,0:T(8,128)(2,1)S(1)}) fusion(f32[512,4096]{1,0:T(8,128)} %fusion.63, f32[4096]{0:T(1024)S(1)} %bitcast.91, bf16[512,1024]{1,0:T(8,128)(2,1)} %param.21, bf16[4096,1024]{1,0:T(8,128)(2,1)} %all-gather.12.cloned.1.call-done), kind=kOutput, calls=%fused_computation.50 | convolution fusion | flops 4341100544 | bytes 22052864 | tf_op jit(solution)/shard_map/dot_general | solution.py:33
  314.0 5.0 multiply_reduce_fusion.1
  319.0 2.7 convert_reduce_fusion.4
  321.7 3.3 fusion.55
  325.2 3.9 convolution_convert_fusion
  330.1 185.8 %while.29 = (s32[]{:T(128)}, bf16[16,512,64]{1,2,0:T(8,128)(2,1)}, f32[16,1024,64]{1,2,0:T(8,128)}, f32[16,1024,64]{1,2,0:T(8,128)}, s32[16]{0:T(128)S(1)}, /*in...) while((s32[]{:T(128)}, bf16[16,512,64]{1,2,0:T(8,128)(2,1)}, ...), condition=%wide.region_15.16_spmd.clone, body=%wide.region_13.15_spmd.clone.sunk | while | flops 343506432 | bytes 17726748 | solution.py:217
  344.5 2.4 multiply_reduce_fusion.7
  402.6 2.4 multiply_reduce_fusion.7
  425.8 2.4 multiply_reduce_fusion.7
  521.7 3.7 collective-permute-start.2
  525.9 8.0 collective-permute-done.3
  534.3 10.8 collective-permute-done.2
  546.6 9.6 fusion.58
  556.3 14.2 %fusion.62 = f32[1024,4096]{1,0:T(8,128)} fusion(bf16[512,4096]{1,0:T(8,128)(2,1)} %copy-done.17, f32[512,1024]{1,0:T(8,128)} %copy-done, f32[1024]{0:T(1024)S(1)} %convert_element_type.117, f32[1024]{0:T(1024)S(1)} %convert_element_type.116, f32[512]{0:T(512)S(1)} %add_rsqrt_fusion, f32[512]{0:T(512)S(1)} %broadcast_multiply_fusion.4), kind=kOutput, calls=%fused_computation.114 | convolution fusion | flops 4297588736 | bytes 23080960 | tf_op jit(solution)/shard_map/dot_general | solution.py:27
  571.0 17.0 %fusion.64 = f32[4096,1024]{1,0:T(8,128)} fusion(bf16[512,1024]{1,0:T(8,128)(2,1)} %param.21, f32[512,4096]{1,0:T(8,128)} %fusion.63, f32[4096]{0:T(1024)S(1)} %bitcast.92), kind=kOutput, calls=%fused_computation.116 | convolution fusion | flops 4315938816 | bytes 26230784 | tf_op jit(solution)/shard_map/dot_general | solution.py:27
  588.0 13.9 %add_convert_fusion.1 = bf16[512,1024]{1,0:T(8,128)(2,1)} fusion(f32[512,1024]{1,0:T(8,128)} %copy-done, bf16[4096,1024]{1,0:T(8,128)(2,1)} %all-gather.12.cloned.1.call-done, f32[1024]{0:T(1024)S(1)} %convert_element_type.121, f32[512,4096]{1,0:T(8,128)} %fusion.63, f32[4096]{0:T(1024)S(1)} %bitcast.93), kind=kOutput, calls=%fused_computation.86 | convolution fusion | flops 4317511680 | bytes 19943424 | tf_op jit(solution)/shard_map/dot_general | solution.py:23
  603.1 8.3 fusion.50
  611.4 41.8 %all-reduce.16 = (f32[1024]{0:T(1024)S(1)}, f32[1024]{0:T(1024)S(1)}, f32[2048]{0:T(1024)S(1)}, f32[1024]{0:T(1024)S(1)}, f32[1024]{0:T(1024)S(1)}, /*index=5*/f...) all-reduce(f32[1024]{0:T(1024)S(1)} %get-tuple-element.203, ...), channel_id=2, replica_groups=mesh['fsdp'=32] {'fsdp'}, use_global_device_ids=true, to_apply=%region_19.20.clone | all-reduce | flops 12288 | bytes 98304
  657.9 3.6 fusion.49
  661.6 49.3 %reduce-scatter.5.cloned.1.call-done = f32[32,3072]{1,0:T(8,128)} async-done(((f32[1024,3072]{1,0:T(8,128)}), f32[32,3072]{1,0:T(8,128)}) %reduce-scatter.5.cloned.1.call-update) | async-done | bytes 393232 | tf_op jit(solution)/shard_map/reduce_scatter | solution.py:247
  710.9 189.0 %reduce-scatter.9.cloned.1.call-done = f32[32,4096]{1,0:T(8,128)} async-done(((f32[1024,4096]{1,0:T(8,128)}), f32[32,4096]{1,0:T(8,128)}) %reduce-scatter.9.cloned.1.call-update) | async-done | bytes 524304 | tf_op jit(solution)/shard_map/reduce_scatter | solution.py:253
  899.9 187.6 %reduce-scatter.11.cloned.1.call-done = f32[128,1024]{1,0:T(8,128)} async-done(((f32[4096,1024]{1,0:T(8,128)}), f32[128,1024]{1,0:T(8,128)}) %reduce-scatter.11.cloned.1.call-update) | async-done | bytes 524304 | tf_op jit(solution)/shard_map/reduce_scatter | solution.py:255
  (348 shorter events, 280.0 us)
Async XLA Ops:
  7.2 49.4 %copy-start.1 = (bf16[512,1024]{1,0:T(8,128)(2,1)S(1)}, bf16[512,1024]{1,0:T(8,128)(2,1)}, u32[]{:S(2)}) copy-start(bf16[512,1024]{1,0:T(8,128)(2,1)} %param.20) | copy-start | bytes 3145732
  7.2 74.6 %all-gather.6.cloned.1.call-start = ((), (), s32[]{:S(2)}) async-start(), calls=%async_computation.4 | async-start | bytes 6488064 | tf_op jit(solution)/shard_map/all_gather | solution.py:85
  7.9 231.3 %all-gather.8.cloned.1.call-start = ((), (), s32[]{:S(2)}) async-start(), calls=%async_computation.5 | async-start | bytes 2162688 | tf_op jit(solution)/shard_map/all_gather | solution.py:87
  8.7 235.2 %all-gather.10.cloned.1.call-start = ((), (), s32[]{:S(2)}) async-start(), calls=%async_computation.6 | async-start | bytes 8650752 | tf_op jit(solution)/shard_map/all_gather | solution.py:91
  9.4 291.3 %all-gather.12.cloned.1.call-start = ((), (), s32[]{:S(2)}) async-start(), calls=%async_computation.7 | async-start | bytes 8650752 | tf_op jit(solution)/shard_map/all_gather | solution.py:93
  88.4 6.0 copy-start.16
  88.4 6.1 copy-start.14
  88.4 54.9 %copy-start.13 = (s32[16384]{0:T(1024)S(1)}, s32[16384]{0:T(1024)}, u32[]{:S(2)}) copy-start(s32[16384]{0:T(1024)} %param.22) | copy-start | bytes 196612
  89.8 53.9 %collective-permute-start = (bf16[512,1024]{1,0:T(8,128)(2,1)S(1)}, bf16[512,1024]{1,0:T(8,128)(2,1)}, u32[]{:S(2)}, u32[]{:S(2)}) collective-permute-start(bf16[512,1024]{1,0:T(8,128)(2,1)S(1)} %get-tuple-element.293), channel_id=1, source_target_pairs={{0,1},{1,2},{2,3},{3,4},{4,5},{5,6},{6,7},{7,8},{8,9},{9,10},{10,1... | collective-permute-start | bytes 3145736 | tf_op jit(solution)/shard_map/ppermute | solution.py:19
  92.1 54.3 %collective-permute-start.1 = (bf16[512,1024]{1,0:T(8,128)(2,1)S(1)}, bf16[512,1024]{1,0:T(8,128)(2,1)}, u32[]{:S(2)}, u32[]{:S(2)}) collective-permute-start(bf16[512,1024]{1,0:T(8,128)(2,1)S(1)} %get-tuple-element.292), channel_id=1, source_target_pairs={{0,1},{1,2},{2,3},{3,4},{4,5},{5,6},{6,7},{7,8},{8,9},{9,10},{10,1... | collective-permute-start | bytes 3145736 | tf_op jit(solution)/shard_map/ppermute | solution.py:19
  94.3 567.3 %reduce-scatter.7.cloned.1.call-start = ((), (), s32[]{:S(2)}) async-start(), calls=%async_computation.9 | async-start | bytes 4325376 | tf_op jit(solution)/shard_map/reduce_scatter | solution.py:249
  239.2 1.0 copy-start.2
  243.5 70.5 %copy-start = (f32[512,1024]{1,0:T(8,128)}, f32[512,1024]{1,0:T(8,128)S(1)}, u32[]{:S(2)}) copy-start(f32[512,1024]{1,0:T(8,128)S(1)} %get-tuple-element.301) | copy-start | bytes 6291460
  300.7 13.2 %copy-start.15 = (bf16[1024,4096]{1,0:T(8,128)(2,1)S(1)}, bf16[1024,4096]{1,0:T(8,128)(2,1)}, u32[]{:S(2)}) copy-start(bf16[1024,4096]{1,0:T(8,128)(2,1)} %all-gather.10.cloned.1.call-done) | copy-start | bytes 25165828
  313.9 5.1 copy-start.17
  313.9 5.1 copy-start.12
  319.0 2.7 copy-start.3
  325.1 385.7 %reduce-scatter.5.cloned.1.call-start = ((), (), s32[]{:S(2)}) async-start(), calls=%async_computation.8 | async-start | bytes 12976128 | tf_op jit(solution)/shard_map/reduce_scatter | solution.py:247
  515.9 9.5 copy-start.11
  517.8 16.1 %collective-permute-start.3 = (bf16[512,1024]{0,1:T(8,128)(2,1)S(1)}, bf16[512,1024]{0,1:T(8,128)(2,1)S(1)}, u32[]{:S(2)}, u32[]{:S(2)}) collective-permute-start(bf16[512,1024]{0,1:T(8,128)(2,1)S(1)} %bitcast.88), channel_id=1, source_target_pairs={{1,0},{2,1},{3,2},{4,3},{5,4},{6,5},{7,6},{8,7},{9,8},{10,9},{11,1... | collective-permute-start | bytes 3145736 | tf_op jit(solution)/shard_map/ppermute | solution.py:19
  521.7 4.0 copy-start.10
  521.7 23.4 %collective-permute-start.2 = (bf16[512,1024]{0,1:T(8,128)(2,1)S(1)}, bf16[512,1024]{0,1:T(8,128)(2,1)S(1)}, u32[]{:S(2)}, u32[]{:S(2)}) collective-permute-start(bf16[512,1024]{0,1:T(8,128)(2,1)S(1)} %bitcast.87), channel_id=1, source_target_pairs={{1,0},{2,1},{3,2},{4,3},{5,4},{6,5},{7,6},{8,7},{9,8},{10,9},{11,1... | collective-permute-start | bytes 3145736 | tf_op jit(solution)/shard_map/ppermute | solution.py:19
  534.3 11.2 %copy-start.6 = (bf16[512,1024]{0,1:T(8,128)(2,1)}, bf16[512,1024]{0,1:T(8,128)(2,1)S(1)}, u32[]{:S(2)}) copy-start(bf16[512,1024]{0,1:T(8,128)(2,1)S(1)} %fusion.53) | copy-start | bytes 3145732
  534.3 12.3 %copy-start.4 = (bf16[16,512,64]{1,2,0:T(8,128)(2,1)S(1)}, bf16[16,512,64]{1,2,0:T(8,128)(2,1)}, u32[]{:S(2)}) copy-start(bf16[16,512,64]{1,2,0:T(8,128)(2,1)} %get-tuple-element.118) | copy-start | bytes 3145732
  545.5 1.1 copy-start.8
  556.2 343.6 %reduce-scatter.9.cloned.1.call-start = ((), (), s32[]{:S(2)}) async-start(), calls=%async_computation.10 | async-start | bytes 17301504 | tf_op jit(solution)/shard_map/reduce_scatter | solution.py:253
  570.5 516.9 %reduce-scatter.11.cloned.1.call-start = ((), (), s32[]{:S(2)}) async-start(), calls=%async_computation.11 | async-start | bytes 17301504 | tf_op jit(solution)/shard_map/reduce_scatter | solution.py:255
  588.0 14.0 %copy-start.5 = (bf16[16,512,64]{1,2,0:T(8,128)(2,1)S(1)}, bf16[16,512,64]{1,2,0:T(8,128)(2,1)}, u32[]{:S(2)}) copy-start(bf16[16,512,64]{1,2,0:T(8,128)(2,1)} %get-tuple-element.118) | copy-start | bytes 3145732
  588.0 14.0 %copy-start.7 = (bf16[512,1024]{0,1:T(8,128)(2,1)S(1)}, bf16[512,1024]{0,1:T(8,128)(2,1)}, u32[]{:S(2)}) copy-start(bf16[512,1024]{0,1:T(8,128)(2,1)} %copy-done.6) | copy-start | bytes 3145732
  588.0 13.9 %copy-start.9 = (bf16[512,1024]{0,1:T(8,128)(2,1)S(1)}, bf16[512,1024]{0,1:T(8,128)(2,1)}, u32[]{:S(2)}) copy-start(bf16[512,1024]{0,1:T(8,128)(2,1)} %copy-done.8) | copy-start | bytes 3145732
Sparse Core Ops, SparseCore 0:
  10.9 70.8 all-gather.5
  84.6 57.7 all-gather.7
  145.2 76.9 all-gather.9
  225.0 75.7 all-gather.11
  325.2 107.7 reduce-scatter.6
  556.4 154.4 reduce-scatter.4
  713.7 186.1 reduce-scatter.8
  902.7 184.6 reduce-scatter.10
where the time goes:
time: 1100 us; the launch traced here: 1090 us
  waiting for transfers between devices  518 us (47%)
  matrix products  330 us (30%)
  blocking collectives  130 us (12%)
  local copies, waits for them, and re-layouts  39.3 us (4%)
  other arithmetic  28.6 us (3%)
  loops' own time  21.9 us (2%)
  between operations  14.9 us (1%)
  starting transfers between devices  11 us (1%)
    reduce_scatter x1, waiting for transfers between devices, on_device(): lax.psum_scatter(fc_w_grad, 'fsdp', scatter_dimension=0, tiled=True)  189 us
    reduce_scatter x1, waiting for transfers between devices, on_device(): lax.psum_scatter(proj_w_grad, 'fsdp', scatter_dimension=0, tiled=True)  188 us
    dot_general x52, matrix products, times_right_t(): lax.dot_general(left, right, (((1,), (1,)), ((), ())), preferred_element_...  127 us
    dot_general x36, matrix products, times_left_t(): lax.dot_general(left, right, (((0,), (0,)), ((), ())), preferred_element_...  109 us
    dot_general x36, matrix products, times_plain(): return jnp.dot(left, right, preferred_element_type=jnp.float32)  95.1 us
    unnamed x2, blocking collectives  81.6 us
    reduce_scatter x1, waiting for transfers between devices, on_device(): lax.psum_scatter(qkv_w_grad, 'fsdp', scatter_dimension=0, tiled=True)  49.3 us
    all_gather x1, blocking collectives, on_device(): lax.all_gather(b_fc, 'fsdp', axis=0, tiled=True)  48.7 us
  transfers between devices with their start and end apart: 12, of which 7 were waited for; matrix products, arithmetic and copies ran while one was open for 34% of the time, Pallas kernels for 0%

commit v1 on v0

v1 whole, which is shorter than its diff:
```python
import functools

import jax
import jax.numpy as jnp
from jax import lax
from jax.experimental import pallas as pl
from jax.experimental.pallas import tpu as pltpu
from jax.sharding import PartitionSpec as P

HEAD_DIM = 64
SEQ = 512
LANES = 128
BLOCK = 256

NORM_EPS = 1e-05
GELU_COEF = 0.7978845608028654
GELU_CUBIC = 0.044715
MASK_FILL = -1e30
SCALE = HEAD_DIM ** (-0.5)


def from_behind(value, axis, steps):
    count = lax.axis_size(axis)
    initial, last = (max(0, -steps), min(count, count - steps))
    return lax.ppermute(value, axis, [(source, source + steps) for source in range(initial, last)])


def times_plain(left, right):
    return jnp.dot(left, right, preferred_element_type=jnp.float32)


def times_left_t(left, right):
    return lax.dot_general(
        left, right, (((0,), (0,)), ((), ())), preferred_element_type=jnp.float32
    )


def times_right_t(left, right):
    return lax.dot_general(
        left, right, (((1,), (1,)), ((), ())), preferred_element_type=jnp.float32
    )


def norm_parts(values):
    centre = jnp.mean(values, axis=-1, keepdims=True)
    centered = values - centre
    inverse = lax.rsqrt(jnp.mean(centered * centered, axis=-1, keepdims=True) + NORM_EPS)
    return (centered * inverse, inverse)


def norm_back(grad_out, normed, inverse, gain_row):
    scaled = grad_out * gain_row
    return inverse * (
        scaled
        - jnp.mean(scaled, axis=-1, keepdims=True)
        - normed * jnp.mean(scaled * normed, axis=-1, keepdims=True)
    )


def one_head(pair, low_lanes, head):
    keep = low_lanes if head == 0 else jnp.logical_not(low_lanes)
    return jnp.where(keep, pair, jnp.zeros_like(pair))


def forward_kernel(bias_ref, q_ref, k_ref, v_ref, pk_ref, pv_ref, out_ref, lse_ref):
    rows = q_ref.shape[0]
    low_lanes = lax.broadcasted_iota(jnp.int32, (1, LANES), 1) < HEAD_DIM
    keys = jnp.concatenate([pk_ref[...], k_ref[...]], axis=0)
    values = jnp.concatenate([pv_ref[...], v_ref[...]], axis=0)
    span = SEQ + BLOCK
    for block in range(rows // BLOCK):
        at = block * BLOCK
        k_block, v_block = keys[at : at + span], values[at : at + span]
        q_pair = q_ref[at : at + BLOCK, :] * jnp.bfloat16(SCALE)
        mixed = []
        for head in range(2):
            scores = times_right_t(k_block, one_head(q_pair, low_lanes, head)) + bias_ref[block]
            top = jnp.max(scores, axis=0, keepdims=True)
            expo = jnp.exp(scores - top)
            total = jnp.sum(expo, axis=0, keepdims=True)
            probs = (expo * (1.0 / total)).astype(jnp.bfloat16)
            mixed.append(times_left_t(probs, v_block))
            lse_ref[0, head : head + 1, at : at + BLOCK] = top + jnp.log(total)
        out_ref[at : at + BLOCK, :] = jnp.where(low_lanes, mixed[0], mixed[1]).astype(jnp.bfloat16)


def backward_kernel(
    bias_ref, q_ref, k_ref, v_ref, pk_ref, pv_ref, g_ref, lse_ref, dq_ref, own_ref, prior_ref, acc
):
    rows = q_ref.shape[0]
    low_lanes = lax.broadcasted_iota(jnp.int32, (1, LANES), 1) < HEAD_DIM
    keys = jnp.concatenate([pk_ref[...], k_ref[...]], axis=0)
    values = jnp.concatenate([pv_ref[...], v_ref[...]], axis=0)
    span = SEQ + BLOCK
    acc[...] = jnp.zeros_like(acc)
    for block in range(rows // BLOCK):
        at = block * BLOCK
        k_block, v_block = keys[at : at + span], values[at : at + span]
        q_pair = q_ref[at : at + BLOCK, :] * jnp.bfloat16(SCALE)
        g_pair = g_ref[at : at + BLOCK, :]
        d_query = jnp.zeros((BLOCK, LANES), jnp.float32)
        d_key = jnp.zeros((span, LANES), jnp.float32)
        d_value = jnp.zeros((span, LANES), jnp.float32)
        for head in range(2):
            q_head = one_head(q_pair, low_lanes, head)
            g_head = one_head(g_pair, low_lanes, head)
            scores = times_right_t(k_block, q_head) + bias_ref[block]
            probs = jnp.exp(scores - lse_ref[0, head : head + 1, at : at + BLOCK])
            d_probs = times_right_t(v_block, g_head)
            delta = jnp.sum(probs * d_probs, axis=0, keepdims=True)
            d_scores = (probs * (d_probs - delta)).astype(jnp.bfloat16)
            d_query = d_query + times_left_t(d_scores, one_head(k_block, low_lanes, head))
            d_key = d_key + times_plain(d_scores, q_head)
            d_value = d_value + times_plain(probs.astype(jnp.bfloat16), g_head)
        dq_ref[at : at + BLOCK, :] = (d_query * SCALE).astype(jnp.bfloat16)
        acc[0, at : at + span, :] += d_key
        acc[1, at : at + span, :] += d_value
    prior_ref[...] = acc[:, :SEQ, :].astype(jnp.bfloat16)
    own_ref[...] = acc[:, SEQ:, :]


def attention_forward(bias, qkv, prior):
    rows, width = qkv.shape[0], qkv.shape[1] // 3
    steps = width // LANES
    column = lambda third: pl.BlockSpec((rows, LANES), lambda h: (0, h + third * steps))
    return pl.pallas_call(
        forward_kernel,
        grid=(steps,),
        in_specs=[
            pl.BlockSpec(bias.shape, lambda h: (0, 0, 0)),
            column(0),
            column(1),
            column(2),
            column(0),
            column(1),
        ],
        out_specs=[column(0), pl.BlockSpec((1, 2, rows), lambda h: (h, 0, 0))],
        out_shape=[
            jax.ShapeDtypeStruct((rows, width), jnp.bfloat16),
            jax.ShapeDtypeStruct((steps, 2, rows), jnp.float32),
        ],
        cost_estimate=pl.CostEstimate(
            flops=8 * rows * width * (SEQ + BLOCK), bytes_accessed=12 * rows * width, transcendentals=0
        ),
        name="attention_forward",
    )(bias, qkv, qkv, qkv, prior, prior)


def attention_backward(bias, qkv, prior, grad_att, lse):
    rows, width = grad_att.shape
    steps = width // LANES
    column = lambda third: pl.BlockSpec((rows, LANES), lambda h: (0, h + third * steps))
    both = pl.BlockSpec((2, rows, LANES), lambda h: (0, 0, h))
    return pl.pallas_call(
        backward_kernel,
        grid=(steps,),
        in_specs=[
            pl.BlockSpec(bias.shape, lambda h: (0, 0, 0)),
            column(0),
            column(1),
            column(2),
            column(0),
            column(1),
            column(0),
            pl.BlockSpec((1, 2, rows), lambda h: (h, 0, 0)),
        ],
        out_specs=[column(0), both, both],
        out_shape=[
            jax.ShapeDtypeStruct((rows, width), jnp.bfloat16),
            jax.ShapeDtypeStruct((2, rows, width), jnp.float32),
            jax.ShapeDtypeStruct((2, SEQ, width), jnp.bfloat16),
        ],
        scratch_shapes=[pltpu.VMEM((2, SEQ + rows, LANES), jnp.float32)],
        cost_estimate=pl.CostEstimate(
            flops=20 * rows * width * (SEQ + BLOCK), bytes_accessed=24 * rows * width, transcendentals=0
        ),
        name="attention_backward",
    )(bias, qkv, qkv, qkv, prior, prior, grad_att, lse)


def score_bias(segments, seq_lengths, first_row, tok_rows):
    seq_ends = jnp.cumsum(seq_lengths)
    position = first_row - SEQ + jnp.arange(SEQ + tok_rows, dtype=jnp.int32)
    padded = jnp.concatenate([jnp.full((SEQ,), -1, jnp.int32), segments])
    segment = lax.dynamic_slice_in_dim(padded, first_row, SEQ + tok_rows, 0)
    sequence = jnp.sum((position[:, None] >= seq_ends[None, :]).astype(jnp.int32), axis=1)
    blocks = []
    for at in range(0, tok_rows, BLOCK):
        key, query = slice(at, at + SEQ + BLOCK), slice(at + SEQ, at + SEQ + BLOCK)
        allowed = segment[key][:, None] == segment[query][None, :]
        allowed = allowed & (sequence[key][:, None] == sequence[query][None, :])
        allowed = allowed & (position[key][:, None] <= position[query][None, :])
        allowed = allowed & (position[key][:, None] >= 0)
        blocks.append(jnp.where(allowed, 0.0, MASK_FILL).astype(jnp.float32))
    return jnp.stack(blocks)


def gather(part):
    return lax.all_gather(part, "fsdp", axis=0, tiled=True)


def scatter(whole):
    return lax.psum_scatter(whole, "fsdp", scatter_dimension=0, tiled=True)


def on_device(
    tokens,
    out_grad,
    segments,
    seq_lengths,
    ln1_gain,
    ln1_bias,
    w_qkv,
    b_qv,
    w_out,
    b_out,
    ln2_gain,
    ln2_bias,
    w_fc,
    b_fc,
    w_proj,
    b_proj,
):
    count = lax.axis_size("fsdp")
    tok_rows, width = tokens.shape
    hidden = w_fc.shape[1]
    share = w_qkv.shape[0]
    folds = hidden // width

    def fold_columns(part):
        return part.reshape(share, count, folds, share).transpose(0, 2, 1, 3).reshape(share, hidden)

    def unfold_columns(part):
        return part.reshape(share, folds, count, share).transpose(0, 2, 1, 3).reshape(share, hidden)

    small = jnp.concatenate(
        [ln1_gain, ln1_bias, b_qv, b_out, ln2_gain, ln2_bias, b_fc, b_proj]
    ).reshape(8 + folds, share)
    small = jnp.pad(small, ((0, LANES - 8 - folds), (0, 0))).T
    first = gather(jnp.concatenate([w_qkv, small], axis=1))
    proj_columns = w_proj.reshape(folds, share, width).transpose(1, 0, 2).reshape(share, hidden)
    second = gather(jnp.concatenate([w_out, fold_columns(w_fc), proj_columns], axis=1))

    qkv_full = first[:, : 3 * width]
    vectors = first[:, 3 * width :].T[: 8 + folds].astype(jnp.float32)
    gain_one, shift_one, out_bias = vectors[0], vectors[1], vectors[4]
    gain_two, shift_two, proj_bias = vectors[5], vectors[6], vectors[7 + folds]
    qv_bias = vectors[2:4].reshape(2, count, share).transpose(1, 0, 2).reshape(2 * width)
    fc_bias = vectors[7 : 7 + folds].reshape(hidden)
    out_full = second[:, :width]
    fc_full = second[:, width : width + hidden]
    proj_full = second[:, width + hidden :]

    first_row = lax.axis_index("fsdp") * tok_rows
    bias = score_bias(segments, seq_lengths, first_row, tok_rows)
    tokens_f = tokens.astype(jnp.float32)
    normed_one, inverse_one = norm_parts(tokens_f)
    hidden_one = (normed_one * gain_one + shift_one).astype(jnp.bfloat16)
    bias_full = jnp.concatenate([qv_bias[:width], jnp.zeros((width,), jnp.float32), qv_bias[width:]])
    qkv = (times_plain(hidden_one, qkv_full) + bias_full).astype(jnp.bfloat16)
    prior = from_behind(qkv[:, width:], "fsdp", 1)
    attended, lse = attention_forward(bias, qkv, prior)

    resid = tokens_f + times_plain(attended, out_full) + out_bias
    normed_two, inverse_two = norm_parts(resid)
    hidden_two = (normed_two * gain_two + shift_two).astype(jnp.bfloat16)
    pre = times_plain(hidden_two, fc_full) + fc_bias
    tanh_part = jnp.tanh(GELU_COEF * (pre + GELU_CUBIC * pre * pre * pre))
    act = (0.5 * pre * (1.0 + tanh_part)).astype(jnp.bfloat16)
    proj_w_grad = jnp.concatenate(
        [
            times_left_t(act[:, j * width : (j + 1) * width], out_grad).astype(jnp.bfloat16)
            for j in range(folds)
        ],
        axis=1,
    )
    proj_share = scatter(proj_w_grad).astype(jnp.float32)
    result = resid + jnp.concatenate([proj_bias[None]], 0)
    for j in range(folds):
        cols = slice(j * width, (j + 1) * width)
        result = result + times_plain(act[:, cols], proj_full[:, cols])
    result = result.astype(jnp.bfloat16)

    grad_top = out_grad.astype(jnp.float32)
    proj_b_grad = jnp.sum(grad_top, axis=0)
    slope = 0.5 * (1.0 + tanh_part) + 0.5 * pre * (1.0 - tanh_part * tanh_part) * GELU_COEF * (
        1.0 + 3.0 * GELU_CUBIC * pre * pre
    )
    grad_act = jnp.concatenate(
        [times_right_t(out_grad, proj_full[:, j * width : (j + 1) * width]) for j in range(folds)],
        axis=1,
    )
    grad_pre = (grad_act * slope).astype(jnp.bfloat16)
    fc_w_grad = times_left_t(hidden_two, grad_pre).astype(jnp.bfloat16)
    fc_b_grad = jnp.sum(grad_pre.astype(jnp.float32), axis=0)
    grad_hidden_two = times_right_t(grad_pre, fc_full)
    gain_two_grad = jnp.sum(grad_hidden_two * normed_two, axis=0)
    shift_two_grad = jnp.sum(grad_hidden_two, axis=0)
    grad_resid = grad_top + norm_back(grad_hidden_two, normed_two, inverse_two, gain_two)
    grad_branch = grad_resid.astype(jnp.bfloat16)
    out_w_grad = times_left_t(attended, grad_branch).astype(jnp.bfloat16)
    out_b_grad = jnp.sum(grad_branch.astype(jnp.float32), axis=0)
    grad_att = times_right_t(grad_branch, out_full).astype(jnp.bfloat16)

    query_grad, own_grads, prior_grads = attention_backward(bias, qkv, prior, grad_att, lse)
    back = from_behind(prior_grads, "fsdp", -1).astype(jnp.float32)
    pair_grads = (own_grads + back).astype(jnp.bfloat16)
    grad_qkv = jnp.concatenate([query_grad, pair_grads[0], pair_grads[1]], axis=1)
    qkv_w_grad = times_left_t(hidden_one, grad_qkv).astype(jnp.bfloat16)
    column_sums = jnp.sum(grad_qkv.astype(jnp.float32), axis=0)
    qv_b_grad = jnp.concatenate([column_sums[:width], column_sums[2 * width :]])
    grad_hidden_one = times_right_t(grad_qkv, qkv_full)
    gain_one_grad = jnp.sum(grad_hidden_one * normed_one, axis=0)
    shift_one_grad = jnp.sum(grad_hidden_one, axis=0)
    tokens_grad = grad_resid + norm_back(grad_hidden_one, normed_one, inverse_one, gain_one)

    vector_grads = jnp.concatenate(
        [
            gain_one_grad[None],
            shift_one_grad[None],
            qv_b_grad.reshape(count, 2, share).transpose(1, 0, 2).reshape(2, width),
            out_b_grad[None],
            gain_two_grad[None],
            shift_two_grad[None],
            fc_b_grad.reshape(folds, width),
            proj_b_grad[None],
        ],
        axis=0,
    ).astype(jnp.bfloat16)
    vector_grads = jnp.pad(vector_grads, ((0, LANES - 8 - folds), (0, 0))).T
    shares = scatter(
        jnp.concatenate([qkv_w_grad, out_w_grad, fc_w_grad, vector_grads], axis=1)
    ).astype(jnp.float32)
    edges = (3 * width, 4 * width, 4 * width + hidden)
    vectors = shares[:, edges[2] :].T[: 8 + folds].reshape(-1)
    at = [share * k for k in (0, 1, 2, 4, 5, 6, 7, 7 + folds, 8 + folds)]
    pieces = [vectors[at[k] : at[k + 1]] for k in range(8)]
    return (
        result,
        tokens_grad,
        pieces[0],
        pieces[1],
        shares[:, : edges[0]],
        pieces[2],
        shares[:, edges[0] : edges[1]],
        pieces[3],
        pieces[4],
        pieces[5],
        unfold_columns(shares[:, edges[1] : edges[2]]),
        pieces[6],
        proj_share.reshape(share, folds, width).transpose(1, 0, 2).reshape(folds * share, width),
        pieces[7],
    )


def solution(mesh):
    rows, flat = P("fsdp", None), P("fsdp")
    return jax.shard_map(
        on_device,
        mesh=mesh,
        in_specs=(rows, rows, P(), P(), flat, flat, rows, flat, rows)
        + (flat, flat, flat, rows, flat, rows, flat),
        out_specs=(rows, rows, flat, flat, rows, flat, rows)
        + (flat, flat, flat, rows, flat, rows, flat),
        check_vma=False,
    )
```

time: 1100 us -> 638 us (0.58)
  matrix products: 330 us -> 92.8 us
  waiting for transfers between devices: 518 us -> 387 us
  blocking collectives: 130 us -> 0 us
  Pallas kernels: 0 us -> 45.9 us
  loops' own time: 21.9 us -> 0 us
  local copies, waits for them, and re-layouts: 39.3 us -> 51 us
    reduce_scatter x4 -> x1, waiting for transfers between devices: 426 us -> 204 us  [scatter(): return lax.psum_scatter(whole, 'fsdp', scatter_dimension=0, tiled=True)]
    dot_general x52 -> x7, matrix products: 127 us -> 33.9 us  [times_right_t(): lax.dot_general(left, right, (((1,), (1,)), ((), ())), preferred_element_...]
    dot_general x36 -> x7, matrix products: 109 us -> 24.8 us  [times_left_t(): lax.dot_general(left, right, (((0,), (0,)), ((), ())), preferred_element_...]
    unnamed x2 -> x0, blocking collectives: 81.6 us -> none
    all_gather x4 -> x2, waiting for transfers between devices: 71.1 us -> 135 us  [gather(): return lax.all_gather(part, 'fsdp', axis=0, tiled=True)]
    dot_general x36 -> x7, matrix products: 95.1 us -> 34.1 us  [times_plain(): return jnp.dot(left, right, preferred_element_type=jnp.float32)]
    all_gather x1 -> x0, blocking collectives: 48.7 us -> none  [on_device(): lax.all_gather(b_fc, 'fsdp', axis=0, tiled=True)]
    pallas_call x0 -> x2, Pallas kernels: none -> 45.9 us  [the longest x1 25.7 us: attention_backward(): pl.pallas_call(backward_kernel, grid=(steps,), in_specs=[pl.BlockSpec(bia...]
  transfers between devices with their start and end apart: 12 -> 6, of which waited for: 7 -> 5; matrix products, arithmetic and copies ran while one was open for 34% -> 19% of each run, Pallas kernels for 0% -> 7%
where the time goes in v1:
time: 638 us; the launch traced here: 630 us
  waiting for transfers between devices  387 us (61%)
  matrix products  92.8 us (15%)
  local copies, waits for them, and re-layouts  51 us (8%)
  Pallas kernels  45.9 us (7%)
  other arithmetic  34.7 us (5%)
  between operations  14.7 us (2%)
    reduce_scatter x1, waiting for transfers between devices, scatter(): return lax.psum_scatter(whole, 'fsdp', scatter_dimension=0, tiled=True)  204 us
    all_gather x2, waiting for transfers between devices, gather(): return lax.all_gather(part, 'fsdp', axis=0, tiled=True)  135 us
    ppermute x2, waiting for transfers between devices, from_behind(): lax.ppermute(value, axis, [(source, source + steps) for source in range(i...  47.5 us
    dot_general x7, matrix products, times_plain(): return jnp.dot(left, right, preferred_element_type=jnp.float32)  34.1 us
    dot_general x7, matrix products, times_right_t(): lax.dot_general(left, right, (((1,), (1,)), ((), ())), preferred_element_...  33.9 us
    pallas_call x1, Pallas kernels, attention_backward(): pl.pallas_call(backward_kernel, grid=(steps,), in_specs=[pl.BlockSpec(bia...  25.7 us
    dot_general x7, matrix products, times_left_t(): lax.dot_general(left, right, (((0,), (0,)), ((), ())), preferred_element_...  24.8 us
    pallas_call x1, Pallas kernels, attention_forward(): pl.pallas_call(forward_kernel, grid=(steps,), in_specs=[pl.BlockSpec(bias...  20.2 us
  transfers between devices with their start and end apart: 6, of which 5 were waited for; matrix products, arithmetic and copies ran while one was open for 19% of the time, Pallas kernels for 7%

profile of v1, /device:TPU:13, one launch (start us, length us, event | category | flops | bytes accessed | tf_op | source)
XLA Modules:
  0.0 630.2 jit_solution(4431264223230617254)
XLA Ops:
  7.2 5.4 concatenate.41
  20.8 65.6 %all-gather.3.cloned.1.call-done = bf16[1024,3200]{1,0:T(8,128)(2,1)} async-done(((bf16[32,3200]{1,0:T(8,128)(2,1)}), bf16[1024,3200]{1,0:T(8,128)(2,1)}) %all-gather.3.cloned.1.call-update) | async-done | bytes 6553616 | tf_op jit(solution)/shard_map/all_gather | solution.py:199
  89.7 6.7 %add_convert_fusion.q_ref.k_ref.v_ref = bf16[512,3072]{1,0:T(8,128)(2,1)S(1)} fusion(bf16[1024,3200]{1,0:T(8,128)(2,1)} %all-gather.3.cloned.1.call-done, f32[3072]{0:T(1024)S(1)} %pad_maximum_fusion.6, bf16[512,1024]{1,0:T(8,128)(2,1)S(1)} %copy-done.1, f32[1024]{0:T(1024)S(1)} %get-tuple-element.36, f32[1024]{0:T(1024)S(1)} %get-tuple-element.37, ...), kind=kOutput, calls=%fused_computation.17 | convolution fusion | flops 3227516928 | bytes 10510336 | tf_op jit(solution)/shard_map/dot_general | solution.py:29
  103.9 27.9 %collective-permute-done.pk_ref.pv_ref = bf16[512,2048]{1,0:T(8,128)(2,1)} collective-permute-done((bf16[512,2048]{1,0:T(8,128)(2,1)}, bf16[512,2048]{1,0:T(8,128)(2,1)}, u32[]{:S(2)}, u32[]{:S(2)}) %collective-permute-start) | collective-permute-done | bytes 2097184 | tf_op jit(solution)/shard_map/ppermute | solution.py:25
  131.8 20.2 %attention_forward.1 = (bf16[512,1024]{1,0:T(8,128)(2,1)}, f32[8,2,512]{2,1,0:T(2,128)}) custom-call(f32[2,768,256]{2,1,0:T(8,128)} %pad_maximum_fusion.3.bias_ref, bf16[512,3072]{1,0:T(8,128)(2,1)} %copy-done, bf16[512,3072]{1,0:T(8,128)(2,1)} %copy-done, bf16[512,3072]{1,0:T(8,128)(2,1)} %copy-done, bf16[512,2048]{1,0:T(8,128)(2,1)} %collective-permute-done.pk_ref.pv_ref, ...), custom_call_target="tpu_custom_call" | custom-call | flops 3221225472 | bytes 6291456 | tf_op jit(solution)/shard_map/attention_forward/pallas_call | solution.py:126
  152.0 69.8 %all-gather.5.cloned.1.call-done = bf16[1024,9216]{1,0:T(8,128)(2,1)} async-done(((bf16[32,9216]{1,0:T(8,128)(2,1)}), bf16[1024,9216]{1,0:T(8,128)(2,1)}) %all-gather.5.cloned.1.call-update) | async-done | bytes 18874384 | tf_op jit(solution)/shard_map/all_gather | solution.py:199
  221.8 3.3 fusion.94
  225.4 11.0 %multiply_convert_fusion = (bf16[512,4096]{1,0:T(8,128)(2,1)S(1)}, f32[512,4096]{1,0:T(8,128)}) fusion(f32[4096]{0:T(1024)S(1)} %bitcast.70, bf16[1024,9216]{1,0:T(8,128)(2,1)} %all-gather.5.cloned.1.call-done, f32[512,1024]{1,0:T(8,128)S(1)} %get-tuple-element.70, f32[1024]{0:T(1024)S(1)} %get-tuple-element.33, f32[1024]{0:T(1024)S(1)} %get-tuple-element.34, ...), kind=kOutput, calls=%fused_computation.11 | convolution fusion | flops 4318560256 | bytes 23097344 | tf_op jit(solution)/shard_map/dot_general | solution.py:29
  241.7 4.2 pad_maximum_fusion.1
  245.9 11.9 %copy.112 = bf16[1024,4096]{1,0:T(8,128)(2,1)} copy(bf16[1024,4096]{0,1:T(8,128)(2,1)} %pad_maximum_fusion.1) | data formatting | bytes 16777216
  257.9 3.2 fusion.52
  261.1 2.9 fusion.55
  264.0 3.0 fusion.58
  267.1 3.1 fusion.61
  270.1 6.4 %fusion.84 = (bf16[4096]{0:T(1024)(128)(2,1)S(1)}, bf16[512,4096]{1,0:T(8,128)(2,1)S(1)}) fusion(f32[512,4096]{1,0:T(8,128)S(1)} %bitcast.60, f32[4096]{0:T(1024)S(1)} %bitcast.71, f32[512,1024]{1,0:T(8,128)S(1)} %fusion.61, f32[512,1024]{1,0:T(8,128)S(1)} %fusion.58, f32[512,1024]{1,0:T(8,128)S(1)} %fusion.55, f32[512,1024]{1,0:T(8,128)S(1)} %fusion.52), kind=kLoop, calls=%fused_computation.136 | loop fusion | flops 50327552 | bytes 20996096 | tf_op jit(solution)/shard_map/reduce_sum | solution.py:295
  276.5 9.1 %multiply_reduce_fusion = (bf16[1024]{0:T(1024)(128)(2,1)S(1)}, f32[512]{0:T(512)S(1)}, f32[512]{0:T(512)S(1)}, bf16[1024]{0:T(1024)(128)(2,1)S(1)}, f32[512,1024]{1,0:T(8,128)S(1)}) fusion(f32[512,1024]{1,0:T(8,128)S(1)} %get-tuple-element.70, f32[512]{0:T(512)S(1)} %add_rsqrt_fusion, f32[512]{0:T(512)S(1)} %broadcast_multiply_fusion.4, ...), kind=kOutput, calls=%fused_computation.44 | convolution fusion | flops 4299682816 | bytes 16793600 | tf_op jit(solution)/shard_map/dot_general | solution.py:39
  286.8 4.6 fusion.64.g_ref
  291.4 25.7 %attention_backward.1 = (bf16[512,1024]{1,0:T(8,128)(2,1)}, f32[2,512,1024]{2,1,0:T(8,128)}, bf16[2,512,1024]{2,1,0:T(8,128)(2,1)}) custom-call(f32[2,768,256]{2,1,0:T(8,128)} %pad_maximum_fusion.3.bias_ref, bf16[512,3072]{1,0:T(8,128)(2,1)} %copy-done, bf16[512,3072]{1,0:T(8,128)(2,1)} %copy-done, bf16[512,3072]{1,0:T(8,128)(2,1)} %copy-done, ...), custom_call_target="tpu_custom_call" | custom-call | flops 8053063680 | bytes 12582912 | tf_op jit(solution)/shard_map/attention_backward/pallas_call | solution.py:154
  319.3 4.6 convolution_convert_fusion.6
  323.9 4.1 copy.103
  328.0 9.3 %convolution_convert_fusion = bf16[1024,4096]{1,0:T(8,128)(2,1)} fusion(bf16[512,4096]{1,0:T(8,128)(2,1)} %copy-done.9, f32[512,1024]{1,0:T(8,128)S(1)} %get-tuple-element.70, f32[1024]{0:T(1024)S(1)} %get-tuple-element.33, f32[1024]{0:T(1024)S(1)} %get-tuple-element.34, f32[512]{0:T(512)S(1)} %add_rsqrt_fusion, f32[512]{0:T(512)S(1)} %broadcast_multiply_fusion.4), kind=kOutput, calls=%fused_computation.12 | convolution fusion | flops 4301783040 | bytes 14692352 | tf_op jit(solution)/shard_map/dot_general | solution.py:33
  337.3 19.6 %collective-permute-done.1 = bf16[2,512,1024]{2,1,0:T(8,128)(2,1)} collective-permute-done((bf16[2,512,1024]{2,1,0:T(8,128)(2,1)}, bf16[2,512,1024]{2,1,0:T(8,128)(2,1)}, u32[]{:S(2)}, u32[]{:S(2)}) %collective-permute-start.1) | collective-permute-done | bytes 2097184 | tf_op jit(solution)/shard_map/ppermute | solution.py:25
  361.0 7.9 %fusion.29 = (bf16[1024]{0:T(1024)(128)(2,1)S(1)}, f32[512]{0:T(512)S(1)}, f32[512]{0:T(512)S(1)}, bf16[1024]{0:T(1024)(128)(2,1)S(1)}, f32[512,1024]{1,0:T(8,128)}) fusion(bf16[512,1024]{1,0:T(8,128)(2,1)S(1)} %copy-done.1, f32[512]{0:T(512)S(1)} %add_rsqrt_fusion.1, f32[512]{0:T(512)S(1)} %broadcast_multiply_fusion.5, f32[1024]{0:T(1024)S(1)} %get-tuple-element.37, ...), kind=kOutput, calls=%fused_computation.40 | convolution fusion | flops 3235902464 | bytes 12599296 | tf_op jit(solution)/shard_map/dot_general | solution.py:39
  370.3 5.7 convolution_convert_fusion.1
  376.0 10.6 %pad_maximum_fusion = bf16[1024,8320]{1,0:T(8,128)(2,1)} fusion(bf16[1024,128]{1,0:T(8,128)(2,1)S(1)} %pad_bitcast_fusion, bf16[1024,4096]{1,0:T(8,128)(2,1)} %convolution_convert_fusion, bf16[1024,1024]{1,0:T(8,128)(2,1)S(1)} %copy-done.2, bf16[1024,3072]{1,0:T(8,128)(2,1)S(1)} %convolution_convert_fusion.1), kind=kLoop, calls=%fused_computation | loop fusion | flops 68157440 | bytes 34078720 | tf_op jit(solution)/shard_map/concatenate | solution.py:332
  386.6 3.3 fusion.34
  390.0 2.9 fusion.38
  392.8 2.9 fusion.42
  395.7 4.1 add_convert_fusion.2
  404.8 203.6 %reduce-scatter.5.cloned.1.call-done = bf16[32,8320]{1,0:T(8,128)(2,1)} async-done(((bf16[1024,8320]{1,0:T(8,128)(2,1)}), bf16[32,8320]{1,0:T(8,128)(2,1)}) %reduce-scatter.5.cloned.1.call-update) | async-done | bytes 532496 | tf_op jit(solution)/shard_map/reduce_scatter | solution.py:203
  614.5 3.1 copy.105
  617.6 4.4 reshape.502
  (145 shorter events, 45.4 us)
Async XLA Ops:
  7.2 79.2 %all-gather.3.cloned.1.call-start = ((), (), s32[]{:S(2)}) async-start(), calls=%async_computation.2 | async-start | bytes 6758400 | tf_op jit(solution)/shard_map/all_gather | solution.py:199
  14.5 207.3 %all-gather.5.cloned.1.call-start = ((), (), s32[]{:S(2)}) async-start(), calls=%async_computation.3 | async-start | bytes 19464192 | tf_op jit(solution)/shard_map/all_gather | solution.py:199
  15.8 3.1 copy-start.16
  17.6 2.3 copy-start.19
  17.6 2.6 copy-start.1
  19.8 382.0 %reduce-scatter.7.cloned.1.call-start = ((), (), s32[]{:S(2)}) async-start(), calls=%async_computation.5 | async-start | bytes 8650752
  96.4 2.5 copy-start
  96.4 4.8 copy-start.17
  98.8 33.0 %collective-permute-start = (bf16[512,2048]{1,0:T(8,128)(2,1)}, bf16[512,2048]{1,0:T(8,128)(2,1)}, u32[]{:S(2)}, u32[]{:S(2)}) collective-permute-start(bf16[512,2048]{1,0:T(8,128)(2,1)} %slice.296), channel_id=1, source_target_pairs={{0,1},{1,2},{2,3},{3,4},{4,5},{5,6},{6,7},{7,8},{8,9},{9,10},{10,1... | collective-permute-start | bytes 6291464 | tf_op jit(solution)/shard_map/ppermute | solution.py:25
  225.4 11.0 %copy-start.11 = (bf16[512,1024]{1,0:T(8,128)(2,1)S(1)}, bf16[512,1024]{1,0:T(8,128)(2,1)}, u32[]{:S(2)}) copy-start(bf16[512,1024]{1,0:T(8,128)(2,1)} %param.17) | copy-start | bytes 3145732
  236.4 3.9 copy-start.14
  257.8 350.6 %reduce-scatter.5.cloned.1.call-start = ((), (), s32[]{:S(2)}) async-start(), calls=%async_computation.4 | async-start | bytes 17571840 | tf_op jit(solution)/shard_map/reduce_scatter | solution.py:203
  257.9 3.3 copy-start.12
  264.0 6.1 slice-start
  267.0 3.1 slice-start.1
  276.5 9.1 %copy-start.9 = (bf16[512,4096]{1,0:T(8,128)(2,1)}, bf16[512,4096]{1,0:T(8,128)(2,1)S(1)}, u32[]{:S(2)}) copy-start(bf16[512,4096]{1,0:T(8,128)(2,1)S(1)} %get-tuple-element.45) | copy-start | bytes 12582916
  286.7 4.6 copy-start.3
  317.1 39.9 %collective-permute-start.1 = (bf16[2,512,1024]{2,1,0:T(8,128)(2,1)}, bf16[2,512,1024]{2,1,0:T(8,128)(2,1)}, u32[]{:S(2)}, u32[]{:S(2)}) collective-permute-start(bf16[2,512,1024]{2,1,0:T(8,128)(2,1)} %get-tuple-element.23), channel_id=1, source_target_pairs={{1,0},{2,1},{3,2},{4,3},{5,4},{6,5},{7,6},{8,7},{9,8},{10,9},{11,1... | collective-permute-start | bytes 6291464 | tf_op jit(solution)/shard_map/ppermute | solution.py:25
  328.0 29.0 %copy-start.6 = (f32[2,512,1024]{2,1,0:T(8,128)S(1)}, f32[2,512,1024]{2,1,0:T(8,128)}, u32[]{:S(2)}) copy-start(f32[2,512,1024]{2,1,0:T(8,128)} %get-tuple-element.22) | copy-start | bytes 12582916
  359.4 1.5 copy-start.13
  359.6 9.3 %copy-start.7 = (bf16[512,1024]{1,0:T(8,128)(2,1)}, bf16[512,1024]{1,0:T(8,128)(2,1)S(1)}, u32[]{:S(2)}) copy-start(bf16[512,1024]{1,0:T(8,128)(2,1)S(1)} %get-tuple-element.48) | copy-start | bytes 3145732
  359.6 9.3 %copy-start.8 = (bf16[512,1024]{1,0:T(8,128)(2,1)}, bf16[512,1024]{1,0:T(8,128)(2,1)S(1)}, u32[]{:S(2)}) copy-start(bf16[512,1024]{1,0:T(8,128)(2,1)S(1)} %get-tuple-element.49) | copy-start | bytes 3145732
  370.3 5.7 copy-start.2
  386.6 3.3 copy-start.15
  392.8 2.9 copy-start.18
  395.7 4.2 copy-start.4
  395.7 4.2 copy-start.10
  608.4 3.5 copy-start.5
Sparse Core Ops, SparseCore 0:
  14.6 71.7 all-gather.2
  89.3 132.4 all-gather.4
  257.9 143.2 reduce-scatter.6
  403.4 205.0 reduce-scatter.4
